TPU v7x, 32 devices: a whole 2x2x4 slice. The times are simulated.
32 devices in a mesh: freq: 4 (over y, x), param: 8 (over z, core).
Axes of the slice: x: 2, y: 2, z: 4, core: 2. Of those that a mesh axis runs over, the one named last changes fastest.
Arguments:
- chain_state: float32 [32, 2048, 512], P('freq', 'param'), may hold values from -6 to 6
- second_moment: float32 [32, 2048, 512], P('freq', 'param'), may hold values from 0.25 to 2
- noise: float32 [2, 32, 2048, 512], P(None, 'freq', 'param'), may hold values from -6 to 6
- green: bfloat16 [2, 64, 2048, 512], P(None, 'freq', 'param'), may hold values from -0.125 to 0.125
- observed: float32 [64, 1024], P('freq'), may hold values from -6 to 6
- inv_noise: float32 [64, 512], P('freq'), may hold values from 0.3 to 3
- temper: float32 [32], P('freq'), may hold values from 0.2 to 1
Outputs:
- new_state: float32 [32, 2048, 512], P('freq', 'param')
- new_moment: float32 [32, 2048, 512], P('freq', 'param')
All inputs are finite; a program needn't handle non-finite values.
Results may differ from a plain program's by a relative error of at most 0.005.
Values may be sent and summed in bfloat16 or wider, within the bound.
A program may use at most 128 MiB of HBM per device.

v0:
```python
import math
import jax
import jax.numpy as jnp
from jax import lax
from jax.sharding import PartitionSpec as P

decay_rate = 0.9
step_length = 0.5


def spectral_table(time_len, freq_total):
    time_index = jnp.arange(time_len, dtype=jnp.int32)[:, None]
    wave_number = jnp.arange(freq_total, dtype=jnp.int32)[None, :] + 1
    phase_angle = (time_index * wave_number % time_len).astype(jnp.float32) * (
        2.0 * math.pi / time_len
    )
    columns_table = jnp.stack([jnp.cos(phase_angle), -jnp.sin(phase_angle)], axis=-1).reshape(
        time_len, 2 * freq_total
    )
    return (columns_table / math.sqrt(time_len)).astype(jnp.bfloat16)


def on_device(chain_state, second_moment, noise, green, observed, inv_noise, temper):
    chains_loc, slab_rows, time_len = chain_state.shape
    freq_loc = green.shape[1]
    freq_count = lax.axis_size("freq")
    freq_total = freq_loc * freq_count
    chains = chains_loc * freq_count
    forward_table = spectral_table(time_len, freq_total)
    inverse_table = forward_table.T
    green_re = green[0]
    green_im = green[1]
    upper_rows = jnp.concatenate([green_re, green_im], axis=2)
    lower_rows = jnp.concatenate([-green_im, green_re], axis=2)
    kernel = jnp.concatenate([upper_rows, lower_rows], axis=1)
    weights = jnp.concatenate([inv_noise, inv_noise], axis=1)
    temper_cols = temper[:, None, None]
    current = chain_state
    moment = second_moment
    for step_num in range(noise.shape[0]):
        low_state = current.astype(jnp.bfloat16)
        local_spec = jnp.dot(
            low_state.reshape(chains_loc * slab_rows, time_len),
            forward_table,
            preferred_element_type=jnp.float32,
        )
        local_spec = local_spec.astype(jnp.bfloat16).reshape(chains_loc, slab_rows, 2 * freq_total)
        spectrum = lax.all_to_all(local_spec, "freq", split_axis=2, concat_axis=0, tiled=True)
        mixed_spec = (
            spectrum.reshape(chains, slab_rows, freq_loc, 2)
            .transpose(2, 0, 3, 1)
            .reshape(freq_loc, chains, 2 * slab_rows)
        )
        partial_data = jnp.einsum(
            "fcq,fqs->fcs", mixed_spec, kernel, preferred_element_type=jnp.float32
        )
        predicted = lax.psum(partial_data.astype(jnp.bfloat16), "param").astype(jnp.float32)
        weighted = (weights[:, None, :] * (predicted - observed[:, None, :])).astype(jnp.bfloat16)
        adjoint = jnp.einsum(
            "fcs,fqs->fcq", weighted, kernel, preferred_element_type=jnp.float32
        ).astype(jnp.bfloat16)
        adjoint = (
            adjoint.reshape(freq_loc, chains, 2, slab_rows)
            .transpose(1, 3, 0, 2)
            .reshape(chains, slab_rows, 2 * freq_loc)
        )
        own_adjoint = lax.all_to_all(adjoint, "freq", split_axis=0, concat_axis=2, tiled=True)
        gradient = jnp.dot(
            own_adjoint.reshape(chains_loc * slab_rows, 2 * freq_total),
            inverse_table,
            preferred_element_type=jnp.float32,
        )
        gradient = gradient.reshape(chains_loc, slab_rows, time_len)
        drift_term = temper_cols * gradient + current
        moment = decay_rate * moment + (1.0 - decay_rate) * drift_term * drift_term
        precondition = lax.rsqrt(moment)
        current = (
            current
            - step_length * precondition * drift_term
            + math.sqrt(2.0 * step_length) * jnp.sqrt(precondition) * noise[step_num]
        )
    return (current, moment)


def solution(mesh):
    return jax.shard_map(
        on_device,
        mesh=mesh,
        in_specs=(
            P("freq", "param", None),
            P("freq", "param", None),
            P(None, "freq", "param", None),
            P(None, "freq", "param", None),
            P("freq", None),
            P("freq", None),
            P("freq"),
        ),
        out_specs=(P("freq", "param", None), P("freq", "param", None)),
        check_vma=False,
    )
```

profile of v0, /device:TPU:0, one launch (start us, length us, event | category | flops | bytes accessed | tf_op | source)
XLA Modules:
  0.0 238.1 jit_solution(13732761810308003860)
XLA Ops:
  7.2 0.6 fusion.19
  7.8 0.1 copy.56
  7.9 0.1 convert_element_type.81
  8.0 2.5 %convert_element_type.82 = bf16[8,256,512]{2,1,0:T(8,128)(2,1)S(1)} convert(f32[8,256,512]{2,1,0:T(8,128)} %param.7) | non-fusion elementwise | flops 1048576 | bytes 6291456 | tf_op jit(solution)/shard_map/convert_element_type | solution.py:41
  10.5 0.8 convolution_convert_fusion.1
  11.3 0.9 copy.86
  12.2 5.2 %all-to-all-start = ((bf16[8,256,128]{1,0,2:T(8,128)(2,1)}), bf16[8,256,128]{1,0,2:T(8,128)(2,1)S(1)}, u32[]{:S(2)}, u32[]{:S(2)}) async-start(bf16[8,256,128]{1,0,2:T(8,128)(2,1)} %bitcast.48), calls=%async_computation | async-start | bytes 1048576 | tf_op jit(solution)/shard_map/all_to_all | solution.py:48
  17.4 0.0 all-reduce.3.cloned.1.call-start
  17.4 5.9 %slice_bitcast_fusion = (bf16[16,256,512]{2,1,0:T(8,128)(2,1)}, bf16[16,256,512]{2,1,0:T(8,128)(2,1)}) fusion(bf16[2,16,256,512]{3,2,1,0:T(8,128)(2,1)} %param.10), kind=kLoop, calls=%fused_computation.11 | loop fusion | bytes 16777216 | tf_op jit(solution)/shard_map/squeeze | solution.py:32
  23.3 4.4 %fusion.20 = bf16[16,256,512]{2,1,0:T(8,128)(2,1)} fusion(bf16[2,16,256,512]{3,2,1,0:T(8,128)(2,1)} %param.10), kind=kLoop, calls=%fused_computation.46 | loop fusion | flops 2097152 | bytes 8388608 | tf_op jit(solution)/shard_map/neg | solution.py:34
  27.7 0.0 all-to-all-done
  27.8 0.0 copy-start.2
  27.8 0.0 copy-start.4
  27.8 8.4 %convolution_convert_fusion.3 = bf16[16,32,1024]{2,1,0:T(8,128)(2,1)} fusion(bf16[16,32,512]{2,1,0:T(8,128)(2,1)S(1)} %bitcast.98, bf16[16,256,512]{2,1,0:T(8,128)(2,1)} %get-tuple-element.7, bf16[16,256,512]{2,1,0:T(8,128)(2,1)} %fusion.20, bf16[16,256,512]{2,1,0:T(8,128)(2,1)} %get-tuple-element.6), kind=kOutput, calls=%fused_computation.18 | convolution fusion | flops 604504064 | bytes 14155776 | tf_op jit(solution)/shard_map/fcq,fqs->fcs/dot_general | solution.py:54
  36.3 0.0 all-reduce.3.cloned.1.call-update
  36.3 0.0 all-reduce.5.cloned.1.call-start
  36.3 0.0 copy-done.2
  36.4 61.1 %all-reduce.3.cloned.1.call-done = bf16[16,32,1024]{2,1,0:T(8,128)(2,1)} async-done(((bf16[16,32,1024]{2,1,0:T(8,128)(2,1)}), bf16[16,32,1024]{2,1,0:T(8,128)(2,1)}) %all-reduce.3.cloned.1.call-update) | async-done | bytes 1048592 | tf_op jit(solution)/shard_map/psum | solution.py:57
  97.5 0.0 copy-done.4
  97.5 8.7 %convolution_convert_fusion.5 = bf16[16,32,512]{2,1,0:T(8,128)(2,1)S(1)} fusion(bf16[16,32,1024]{2,1,0:T(8,128)(2,1)} %all-reduce.3.cloned.1.call-done, f32[16,1024]{1,0:T(8,128)S(1)} %copy-done.4, f32[16,1024]{1,0:T(8,128)S(1)} %pad_maximum_fusion, bf16[16,256,512]{2,1,0:T(8,128)(2,1)} %get-tuple-element.7, bf16[16,256,512]{2,1,0:T(8,128)(2,1)} %fusion.20, ...), kind=kOutput, calls=%fused_computation.20 | convolution fusion | flops 606339072 | bytes 14286848 | tf_op jit(solution)/shard_map/fcs,fqs->fcq/dot_general | solution.py:59
  106.2 0.0 copy-start
  106.2 0.0 copy-start.3
  106.3 0.1 copy.92
  106.3 0.3 copy.61
  106.6 10.8 %all_to_all.60 = bf16[32,256,32]{1,2,0:T(8,128)(2,1)S(1)} all-to-all(bf16[32,256,32]{1,2,0:T(8,128)(2,1)S(1)} %copy.61), channel_id=1, replica_groups=mesh['freq'=4,'param'=8] {'freq'}, dimensions={0} | all-to-all | bytes 1048576 | tf_op jit(solution)/shard_map/all_to_all | solution.py:67
  117.4 0.0 copy-done
  117.5 0.0 copy-done.3
  117.5 7.4 %fusion.22 = (bf16[8,256,512]{2,1,0:T(8,128)(2,1)S(1)}, f32[8,256,512]{2,1,0:T(8,128)}, f32[8,256,512]{2,1,0:T(8,128)}) fusion(f32[2,8,256,512]{3,2,1,0:T(8,128)} %param.9, f32[8,256,512]{2,1,0:T(8,128)S(1)} %copy-done, f32[8]{0:T(128)S(1)} %copy-done.3, f32[8,256,512]{2,1,0:T(8,128)} %param.8, bf16[8,256,128]{1,2,0:T(8,128)(2,1)S(1)} %bitcast.88, ...), kind=kOutput, calls=%fused_computation.47 | convolution fusion | flops 281018368 | bytes 23724064 | tf_op jit(solution)/shard_map/dot_general | solution.py:68
  124.8 0.7 convolution_convert_fusion
  125.5 0.4 copy.65
  125.9 9.5 %all_to_all.61 = bf16[8,256,128]{1,0,2:T(8,128)(2,1)S(1)} all-to-all(bf16[8,256,128]{1,0,2:T(8,128)(2,1)S(1)} %copy.65), channel_id=1, replica_groups=mesh['freq'=4,'param'=8] {'freq'}, dimensions={2} | all-to-all | bytes 1048576 | tf_op jit(solution)/shard_map/all_to_all | solution.py:48
  135.5 8.4 %convolution_convert_fusion.2 = bf16[16,32,1024]{2,1,0:T(8,128)(2,1)} fusion(bf16[16,32,512]{2,1,0:T(8,128)(2,1)S(1)} %bitcast.100, bf16[16,256,512]{2,1,0:T(8,128)(2,1)} %get-tuple-element.7, bf16[16,256,512]{2,1,0:T(8,128)(2,1)} %fusion.20, bf16[16,256,512]{2,1,0:T(8,128)(2,1)} %get-tuple-element.6), kind=kOutput, calls=%fused_computation.17 | convolution fusion | flops 604504064 | bytes 14155776 | tf_op jit(solution)/shard_map/fcq,fqs->fcs/dot_general | solution.py:54
  143.9 0.0 all-reduce.5.cloned.1.call-update
  144.0 57.5 %all-reduce.5.cloned.1.call-done = bf16[16,32,1024]{2,1,0:T(8,128)(2,1)} async-done(((bf16[16,32,1024]{2,1,0:T(8,128)(2,1)}), bf16[16,32,1024]{2,1,0:T(8,128)(2,1)}) %all-reduce.5.cloned.1.call-update) | async-done | bytes 1048592 | tf_op jit(solution)/shard_map/psum | solution.py:57
  201.5 8.8 %convolution_convert_fusion.4 = bf16[16,32,512]{2,1,0:T(8,128)(2,1)S(1)} fusion(bf16[16,32,1024]{2,1,0:T(8,128)(2,1)} %all-reduce.5.cloned.1.call-done, f32[16,1024]{1,0:T(8,128)S(1)} %copy-done.4, f32[16,1024]{1,0:T(8,128)S(1)} %pad_maximum_fusion, bf16[16,256,512]{2,1,0:T(8,128)(2,1)} %get-tuple-element.7, bf16[16,256,512]{2,1,0:T(8,128)(2,1)} %fusion.20, ...), kind=kOutput, calls=%fused_computation.19 | convolution fusion | flops 606339072 | bytes 14286848 | tf_op jit(solution)/shard_map/fcs,fqs->fcq/dot_general | solution.py:59
  210.3 0.0 copy-start.1
  210.3 0.1 copy.91
  210.4 0.3 copy.70
  210.7 10.8 %all_to_all.62 = bf16[32,256,32]{1,2,0:T(8,128)(2,1)S(1)} all-to-all(bf16[32,256,32]{1,2,0:T(8,128)(2,1)S(1)} %copy.70), channel_id=1, replica_groups=mesh['freq'=4,'param'=8] {'freq'}, dimensions={0} | all-to-all | bytes 1048576 | tf_op jit(solution)/shard_map/all_to_all | solution.py:67
  221.5 0.0 copy-done.1
  221.5 9.7 %fusion.2 = (f32[8,256,512]{2,1,0:T(8,128)}, f32[8,256,512]{2,1,0:T(8,128)}) fusion(f32[2,8,256,512]{3,2,1,0:T(8,128)} %param.9, f32[8,256,512]{2,1,0:T(8,128)} %get-tuple-element.5, f32[8]{0:T(128)S(1)} %copy-done.3, f32[8,256,512]{2,1,0:T(8,128)S(1)} %copy-done.1, f32[8,256,512]{2,1,0:T(8,128)} %get-tuple-element.10, f32[8,256,512]{2,1,0:T(8,128)} %param.8, ...), kind=kOutput, calls=%fused_computation.6 | convolution fusion | flops 286261248 | bytes 30015520 | tf_op jit(solution)/shard_map/dot_general | solution.py:68
  (7 shorter events, 0.2 us)
Async XLA Ops:
  12.2 15.5 %all-to-all-start = ((bf16[8,256,128]{1,0,2:T(8,128)(2,1)}), bf16[8,256,128]{1,0,2:T(8,128)(2,1)S(1)}, u32[]{:S(2)}, u32[]{:S(2)}) async-start(bf16[8,256,128]{1,0,2:T(8,128)(2,1)} %bitcast.48), calls=%async_computation | async-start | bytes 1048576 | tf_op jit(solution)/shard_map/all_to_all | solution.py:48
  17.4 80.1 %all-reduce.3.cloned.1.call-start = ((), (), s32[]{:S(2)}) async-start(), calls=%async_computation.4 | async-start | bytes 2097152 | tf_op jit(solution)/shard_map/psum | solution.py:57
  27.8 8.5 %copy-start.2 = (f32[16,512]{1,0:T(8,128)S(1)}, f32[16,512]{1,0:T(8,128)}, u32[]{:S(2)}) copy-start(f32[16,512]{1,0:T(8,128)} %param.12) | copy-start | bytes 98308
  27.8 69.7 %copy-start.4 = (f32[16,1024]{1,0:T(8,128)S(1)}, f32[16,1024]{1,0:T(8,128)}, u32[]{:S(2)}) copy-start(f32[16,1024]{1,0:T(8,128)} %param.11) | copy-start | bytes 196612
  36.3 165.2 %all-reduce.5.cloned.1.call-start = ((), (), s32[]{:S(2)}) async-start(), calls=%async_computation.5 | async-start | bytes 2097152 | tf_op jit(solution)/shard_map/psum | solution.py:57
  106.2 11.2 %copy-start = (f32[8,256,512]{2,1,0:T(8,128)S(1)}, f32[8,256,512]{2,1,0:T(8,128)}, u32[]{:S(2)}) copy-start(f32[8,256,512]{2,1,0:T(8,128)} %param.7) | copy-start | bytes 12582916
  106.2 11.2 %copy-start.3 = (f32[8]{0:T(128)S(1)}, f32[8]{0:T(128)}, u32[]{:S(2)}) copy-start(f32[8]{0:T(128)} %param.13) | copy-start | bytes 100
  210.3 11.2 %copy-start.1 = (f32[8,256,512]{2,1,0:T(8,128)S(1)}, f32[8,256,512]{2,1,0:T(8,128)}, u32[]{:S(2)}) copy-start(f32[8,256,512]{2,1,0:T(8,128)} %param.7) | copy-start | bytes 12582916
Sparse Core Ops, SparseCore 0:
  36.4 61.0 all-reduce.2
  144.1 57.3 all-reduce.4
where the time goes:
time: 238 us
  waiting for transfers between devices  119 us (50%)
  matrix products  53.1 us (22%)
  blocking collectives  31.1 us (13%)
  between operations  14.2 us (6%)
  local copies, waits for them, and re-layouts  8.32 us (3%)
  other arithmetic  7.49 us (3%)
  starting transfers between devices  5.23 us (2%)
    psum x2, waiting for transfers between devices, on_device(): lax.psum(partial_data.astype(jnp.bfloat16), 'param').astype(jnp.float32)  119 us
    all_to_all x2, blocking collectives, on_device(): lax.all_to_all(adjoint, 'freq', split_axis=0, concat_axis=2, tiled=True)  21.6 us
    dot_general x2, matrix products, on_device(): jnp.einsum('fcs,fqs->fcq', weighted, kernel, preferred_element_type=jnp.f...  17.6 us
    dot_general x2, matrix products, on_device(): jnp.dot(own_adjoint.reshape(chains_loc * slab_rows, 2 * freq_total), inve...  17.1 us
    dot_general x2, matrix products, on_device(): jnp.einsum('fcq,fqs->fcs', mixed_spec, kernel, preferred_element_type=jnp...  16.9 us
    all_to_all x1, blocking collectives, on_device(): lax.all_to_all(local_spec, 'freq', split_axis=2, concat_axis=0, tiled=True)  9.53 us
    squeeze x1, local copies, waits for them, and re-layouts, on_device(): green_im = green[1]  5.93 us
    all_to_all x1, starting transfers between devices, on_device(): lax.all_to_all(local_spec, 'freq', split_axis=2, concat_axis=0, tiled=True)  5.19 us
  transfers between devices with their start and end apart: 3, of which 2 were waited for; matrix products, arithmetic and copies ran while one was open for 4% of the time, Pallas kernels for 0%

commit v1 on v0

--- a/solution.py
+++ b/solution.py
@@ -54,7 +54,9 @@
         partial_data = jnp.einsum(
             "fcq,fqs->fcs", mixed_spec, kernel, preferred_element_type=jnp.float32
         )
-        predicted = lax.psum(partial_data.astype(jnp.bfloat16), "param").astype(jnp.float32)
+        predicted = jnp.sum(
+            lax.all_gather(partial_data.astype(jnp.bfloat16), "param"), axis=0
+        ).astype(jnp.float32)
         weighted = (weights[:, None, :] * (predicted - observed[:, None, :])).astype(jnp.bfloat16)
         adjoint = jnp.einsum(
             "fcs,fqs->fcq", weighted, kernel, preferred_element_type=jnp.float32

time: 238 us -> 298 us (1.25)
  waiting for transfers between devices: 119 us -> 163 us
  other arithmetic: 7.49 us -> 18.6 us
  blocking collectives: 31.1 us -> 35.4 us
    all_gather x0 -> x2, waiting for transfers between devices: none -> 163 us  [on_device(): lax.all_gather(partial_data.astype(jnp.bfloat16), 'param')]
    psum x2 -> x0, waiting for transfers between devices: 119 us -> none  [on_device(): lax.psum(partial_data.astype(jnp.bfloat16), 'param').astype(jnp.float32)]
    reduce_sum x0 -> x2, other arithmetic: none -> 11.1 us  [on_device(): jnp.sum(lax.all_gather(partial_data.astype(jnp.bfloat16), 'param'), axis=0)]
    all_to_all x2, blocking collectives: 21.6 us -> 25.3 us  [on_device(): lax.all_to_all(adjoint, 'freq', split_axis=0, concat_axis=2, tiled=True)]
  transfers between devices with their start and end apart: 3 -> 3, of which waited for: 2 -> 2; matrix products, arithmetic and copies ran while one was open for 4% -> 3% of each run, Pallas kernels for 0% -> 0%
where the time goes in v1:
time: 298 us; the launch traced here: 297 us
  waiting for transfers between devices  163 us (55%)
  matrix products  52.3 us (18%)
  blocking collectives  35.4 us (12%)
  other arithmetic  18.6 us (6%)
  between operations  14.3 us (5%)
  local copies, waits for them, and re-layouts  8.31 us (3%)
  starting transfers between devices  5.23 us (2%)
    all_gather x2, waiting for transfers between devices, on_device(): lax.all_gather(partial_data.astype(jnp.bfloat16), 'param')  163 us
    all_to_all x2, blocking collectives, on_device(): lax.all_to_all(adjoint, 'freq', split_axis=0, concat_axis=2, tiled=True)  25.3 us
    dot_general x2, matrix products, on_device(): jnp.einsum('fcs,fqs->fcq', weighted, kernel, preferred_element_type=jnp.f...  17.2 us
    dot_general x2, matrix products, on_device(): jnp.dot(own_adjoint.reshape(chains_loc * slab_rows, 2 * freq_total), inve...  17 us
    dot_general x2, matrix products, on_device(): jnp.einsum('fcq,fqs->fcs', mixed_spec, kernel, preferred_element_type=jnp...  16.6 us
    reduce_sum x2, other arithmetic, on_device(): jnp.sum(lax.all_gather(partial_data.astype(jnp.bfloat16), 'param'), axis=0)  11.1 us
    all_to_all x1, blocking collectives, on_device(): lax.all_to_all(local_spec, 'freq', split_axis=2, concat_axis=0, tiled=True)  10.1 us
  transfers between devices with their start and end apart: 3, of which 2 were waited for; matrix products, arithmetic and copies ran while one was open for 3% of the time, Pallas kernels for 0%

profile of v1, /device:TPU:0, one launch (start us, length us, event | category | flops | bytes accessed | tf_op | source)
XLA Modules:
  0.0 297.2 jit_solution(3764874065682101320)
XLA Ops:
  7.2 0.6 fusion.19
  7.8 0.1 copy.56
  7.9 0.1 convert_element_type.85
  8.0 2.5 convert_element_type.86
  10.5 0.8 convolution_convert_fusion.1
  11.3 0.9 copy.86
  12.2 5.2 %all-to-all-start = ((bf16[8,256,128]{1,0,2:T(8,128)(2,1)}), bf16[8,256,128]{1,0,2:T(8,128)(2,1)S(1)}, u32[]{:S(2)}, u32[]{:S(2)}) async-start(bf16[8,256,128]{1,0,2:T(8,128)(2,1)} %bitcast.50), calls=%async_computation | async-start | bytes 1048576 | tf_op jit(solution)/shard_map/all_to_all | solution.py:48
  17.4 0.0 all-gather.5.cloned.1.call-start
  17.4 5.9 %slice_bitcast_fusion = (bf16[16,256,512]{2,1,0:T(8,128)(2,1)}, bf16[16,256,512]{2,1,0:T(8,128)(2,1)}) fusion(bf16[2,16,256,512]{3,2,1,0:T(8,128)(2,1)} %param.10), kind=kLoop, calls=%fused_computation.11 | loop fusion | bytes 16777216 | tf_op jit(solution)/shard_map/squeeze | solution.py:32
  23.3 4.4 %fusion.20 = bf16[16,256,512]{2,1,0:T(8,128)(2,1)} fusion(bf16[2,16,256,512]{3,2,1,0:T(8,128)(2,1)} %param.10), kind=kLoop, calls=%fused_computation.46 | loop fusion | flops 2097152 | bytes 8388608 | tf_op jit(solution)/shard_map/neg | solution.py:34
  27.7 0.0 all-to-all-done
  27.8 0.0 copy-start.2
  27.8 8.3 %convolution_convert_fusion.3 = bf16[16,32,1024]{2,1,0:T(8,128)(2,1)} fusion(bf16[16,32,512]{2,1,0:T(8,128)(2,1)S(1)} %bitcast.102, bf16[16,256,512]{2,1,0:T(8,128)(2,1)} %get-tuple-element.7, bf16[16,256,512]{2,1,0:T(8,128)(2,1)} %fusion.20, bf16[16,256,512]{2,1,0:T(8,128)(2,1)} %get-tuple-element.6), kind=kOutput, calls=%fused_computation.18 | convolution fusion | flops 604504064 | bytes 14155776 | tf_op jit(solution)/shard_map/fcq,fqs->fcs/dot_general | solution.py:54
  36.1 0.0 all-gather.5.cloned.1.call-update
  36.2 0.0 all-gather.7.cloned.1.call-start
  36.2 0.0 copy-done.2
  36.2 83.9 %all-gather.5.cloned.1.call-done = bf16[128,32,1024]{2,1,0:T(8,128)(2,1)} async-done(((bf16[16,32,1024]{2,1,0:T(8,128)(2,1)}), bf16[128,32,1024]{2,1,0:T(8,128)(2,1)}) %all-gather.5.cloned.1.call-update) | async-done | bytes 8388624 | tf_op jit(solution)/shard_map/all_gather | solution.py:58
  120.1 0.0 copy-start.4
  120.1 5.6 %reduce_sum.24 = bf16[16,32,1024]{2,1,0:T(8,128)(2,1)S(1)} reduce(bf16[8,16,32,1024]{3,2,1,0:T(8,128)(2,1)} %bitcast.89, bf16[]{:T(256)} %constant.29.clone.1), dimensions={0}, to_apply=%region_0.1 | reduce | flops 3670016 | bytes 9437186 | tf_op jit(solution)/shard_map/reduce_sum | solution.py:57
  125.7 0.0 copy-done.4
  125.7 8.6 %convolution_convert_fusion.5 = bf16[16,32,512]{2,1,0:T(8,128)(2,1)S(1)} fusion(bf16[16,32,1024]{2,1,0:T(8,128)(2,1)S(1)} %reduce_sum.24, f32[16,1024]{1,0:T(8,128)S(1)} %copy-done.4, f32[16,1024]{1,0:T(8,128)S(1)} %pad_maximum_fusion, bf16[16,256,512]{2,1,0:T(8,128)(2,1)} %get-tuple-element.7, bf16[16,256,512]{2,1,0:T(8,128)(2,1)} %fusion.20, ...), kind=kOutput, calls=%fused_computation.20 | convolution fusion | flops 606339072 | bytes 14286848 | tf_op jit(solution)/shard_map/fcs,fqs->fcq/dot_general | solution.py:61
  134.3 0.0 copy-start
  134.3 0.0 copy-start.3
  134.3 0.1 copy.92
  134.4 0.3 copy.61
  134.7 12.6 %all_to_all.60 = bf16[32,256,32]{1,2,0:T(8,128)(2,1)S(1)} all-to-all(bf16[32,256,32]{1,2,0:T(8,128)(2,1)S(1)} %copy.61), channel_id=1, replica_groups=mesh['freq'=4,'param'=8] {'freq'}, dimensions={0} | all-to-all | bytes 1048576 | tf_op jit(solution)/shard_map/all_to_all | solution.py:69
  147.3 0.0 copy-done
  147.4 0.0 copy-done.3
  147.4 7.3 %fusion.22 = (bf16[8,256,512]{2,1,0:T(8,128)(2,1)S(1)}, f32[8,256,512]{2,1,0:T(8,128)}, f32[8,256,512]{2,1,0:T(8,128)}) fusion(f32[2,8,256,512]{3,2,1,0:T(8,128)} %param.9, f32[8,256,512]{2,1,0:T(8,128)S(1)} %copy-done, f32[8]{0:T(128)S(1)} %copy-done.3, f32[8,256,512]{2,1,0:T(8,128)} %param.8, bf16[8,256,128]{1,2,0:T(8,128)(2,1)S(1)} %bitcast.92, ...), kind=kOutput, calls=%fused_computation.47 | convolution fusion | flops 281018368 | bytes 23724064 | tf_op jit(solution)/shard_map/dot_general | solution.py:70
  154.6 0.7 convolution_convert_fusion
  155.3 0.4 copy.65
  155.7 10.1 %all_to_all.61 = bf16[8,256,128]{1,0,2:T(8,128)(2,1)S(1)} all-to-all(bf16[8,256,128]{1,0,2:T(8,128)(2,1)S(1)} %copy.65), channel_id=1, replica_groups=mesh['freq'=4,'param'=8] {'freq'}, dimensions={2} | all-to-all | bytes 1048576 | tf_op jit(solution)/shard_map/all_to_all | solution.py:48
  165.9 8.3 %convolution_convert_fusion.2 = bf16[16,32,1024]{2,1,0:T(8,128)(2,1)} fusion(bf16[16,32,512]{2,1,0:T(8,128)(2,1)S(1)} %bitcast.104, bf16[16,256,512]{2,1,0:T(8,128)(2,1)} %get-tuple-element.7, bf16[16,256,512]{2,1,0:T(8,128)(2,1)} %fusion.20, bf16[16,256,512]{2,1,0:T(8,128)(2,1)} %get-tuple-element.6), kind=kOutput, calls=%fused_computation.17 | convolution fusion | flops 604504064 | bytes 14155776 | tf_op jit(solution)/shard_map/fcq,fqs->fcs/dot_general | solution.py:54
  174.2 0.0 all-gather.7.cloned.1.call-update
  174.2 79.2 %all-gather.7.cloned.1.call-done = bf16[128,32,1024]{2,1,0:T(8,128)(2,1)} async-done(((bf16[16,32,1024]{2,1,0:T(8,128)(2,1)}), bf16[128,32,1024]{2,1,0:T(8,128)(2,1)}) %all-gather.7.cloned.1.call-update) | async-done | bytes 8388624 | tf_op jit(solution)/shard_map/all_gather | solution.py:58
  253.4 5.5 %reduce_sum.25 = bf16[16,32,1024]{2,1,0:T(8,128)(2,1)S(1)} reduce(bf16[8,16,32,1024]{3,2,1,0:T(8,128)(2,1)} %bitcast.90, bf16[]{:T(256)} %constant.29.clone.1), dimensions={0}, to_apply=%region_1.2 | reduce | flops 3670016 | bytes 9437186 | tf_op jit(solution)/shard_map/reduce_sum | solution.py:57
  259.0 8.6 %convolution_convert_fusion.4 = bf16[16,32,512]{2,1,0:T(8,128)(2,1)S(1)} fusion(bf16[16,32,1024]{2,1,0:T(8,128)(2,1)S(1)} %reduce_sum.25, f32[16,1024]{1,0:T(8,128)S(1)} %copy-done.4, f32[16,1024]{1,0:T(8,128)S(1)} %pad_maximum_fusion, bf16[16,256,512]{2,1,0:T(8,128)(2,1)} %get-tuple-element.7, bf16[16,256,512]{2,1,0:T(8,128)(2,1)} %fusion.20, ...), kind=kOutput, calls=%fused_computation.19 | convolution fusion | flops 606339072 | bytes 14286848 | tf_op jit(solution)/shard_map/fcs,fqs->fcq/dot_general | solution.py:61
  267.6 0.0 copy-start.1
  267.6 0.1 copy.91
  267.7 0.3 copy.70
  268.0 12.6 %all_to_all.62 = bf16[32,256,32]{1,2,0:T(8,128)(2,1)S(1)} all-to-all(bf16[32,256,32]{1,2,0:T(8,128)(2,1)S(1)} %copy.70), channel_id=1, replica_groups=mesh['freq'=4,'param'=8] {'freq'}, dimensions={0} | all-to-all | bytes 1048576 | tf_op jit(solution)/shard_map/all_to_all | solution.py:69
  280.6 0.0 copy-done.1
  280.6 9.7 %fusion.2 = (f32[8,256,512]{2,1,0:T(8,128)}, f32[8,256,512]{2,1,0:T(8,128)}) fusion(f32[2,8,256,512]{3,2,1,0:T(8,128)} %param.9, f32[8,256,512]{2,1,0:T(8,128)} %get-tuple-element.5, f32[8]{0:T(128)S(1)} %copy-done.3, f32[8,256,512]{2,1,0:T(8,128)S(1)} %copy-done.1, f32[8,256,512]{2,1,0:T(8,128)} %get-tuple-element.10, f32[8,256,512]{2,1,0:T(8,128)} %param.8, ...), kind=kOutput, calls=%fused_computation.6 | convolution fusion | flops 286261248 | bytes 30015520 | tf_op jit(solution)/shard_map/dot_general | solution.py:70
  (7 shorter events, 0.2 us)
Async XLA Ops:
  12.2 15.5 %all-to-all-start = ((bf16[8,256,128]{1,0,2:T(8,128)(2,1)}), bf16[8,256,128]{1,0,2:T(8,128)(2,1)S(1)}, u32[]{:S(2)}, u32[]{:S(2)}) async-start(bf16[8,256,128]{1,0,2:T(8,128)(2,1)} %bitcast.50), calls=%async_computation | async-start | bytes 1048576 | tf_op jit(solution)/shard_map/all_to_all | solution.py:48
  17.4 102.7 %all-gather.5.cloned.1.call-start = ((), (), s32[]{:S(2)}) async-start(), calls=%async_computation.4 | async-start | bytes 9437184 | tf_op jit(solution)/shard_map/all_gather | solution.py:58
  27.8 8.4 %copy-start.2 = (f32[16,512]{1,0:T(8,128)S(1)}, f32[16,512]{1,0:T(8,128)}, u32[]{:S(2)}) copy-start(f32[16,512]{1,0:T(8,128)} %param.12) | copy-start | bytes 98308
  36.2 217.3 %all-gather.7.cloned.1.call-start = ((), (), s32[]{:S(2)}) async-start(), calls=%async_computation.5 | async-start | bytes 9437184 | tf_op jit(solution)/shard_map/all_gather | solution.py:58
  120.1 5.6 %copy-start.4 = (f32[16,1024]{1,0:T(8,128)S(1)}, f32[16,1024]{1,0:T(8,128)}, u32[]{:S(2)}) copy-start(f32[16,1024]{1,0:T(8,128)} %param.11) | copy-start | bytes 196612
  134.3 13.1 %copy-start = (f32[8,256,512]{2,1,0:T(8,128)S(1)}, f32[8,256,512]{2,1,0:T(8,128)}, u32[]{:S(2)}) copy-start(f32[8,256,512]{2,1,0:T(8,128)} %param.7) | copy-start | bytes 12582916
  134.3 13.1 %copy-start.3 = (f32[8]{0:T(128)S(1)}, f32[8]{0:T(128)}, u32[]{:S(2)}) copy-start(f32[8]{0:T(128)} %param.13) | copy-start | bytes 100
  267.6 13.1 %copy-start.1 = (f32[8,256,512]{2,1,0:T(8,128)S(1)}, f32[8,256,512]{2,1,0:T(8,128)}, u32[]{:S(2)}) copy-start(f32[8,256,512]{2,1,0:T(8,128)} %param.7) | copy-start | bytes 12582916
Sparse Core Ops, SparseCore 0:
  36.3 83.7 all-gather.4
  174.3 79.0 all-gather.6
